TPU v7x, 32 devices: a whole 2x2x4 slice. The times are simulated.
32 devices in a mesh: seq: 8 (over z, x), ep: 4 (over y, core).
Axes of the slice: x: 2, y: 2, z: 4, core: 2. Of those that a mesh axis runs over, the one named last changes fastest.
Arguments:
- tokens: bfloat16 [1024, 2048], P('seq'), may hold values from -12 to 12
- attn_gain: float32 [2048], replicated, may hold values from 0.1 to 1.9
- w_query: bfloat16 [2048, 512], P(None, 'ep'), may hold values from -1 to 1
- w_key: bfloat16 [2048, 512], P(None, 'ep'), may hold values from -8 to 8
- w_value: bfloat16 [2048, 512], P(None, 'ep'), may hold values from -0.125 to 0.125
- w_out: bfloat16 [512, 2048], P('ep'), may hold values from -0.25 to 0.25
- moe_gain: float32 [2048], replicated, may hold values from 0.1 to 1.9
- expert_ids: int32 [1024, 6], P('seq'), may hold values from 0 to 15, all different within a row; in each aligned block of 128 rows (0 to 127, 128 to 255, ...) at most 52 rows name the same one
- route_weight: float32 [1024, 6], P('seq'), may hold values from 0.2 to 1
- w_gate: bfloat16 [5632, 2048], P(('seq', 'ep')), may hold values from -0.125 to 0.125
- w_up: bfloat16 [5632, 2048], P(('seq', 'ep')), may hold values from -0.125 to 0.125
- w_down: bfloat16 [5632, 2048], P(('seq', 'ep')), may hold values from -0.3125 to 0.3125
Outputs:
- layer_out: bfloat16 [1024, 2048], P(('seq', 'ep'))
Inputs may be any that keep to these rules, and one draw needn't show every extreme that they name: `expert_ids`: each frame names 6 different experts; among the frames of one block of 128 no expert is named by more than 52 frames, a bound that some block reaches.
All inputs are finite; a program needn't handle non-finite values.
Results may differ from a plain program's by a relative error of at most 0.0065.
Values may be sent and summed in bfloat16 or wider, within the bound.
A program may use at most 64 MiB of HBM per device.

v0:
```python
import math

import jax
import jax.numpy as jnp
from jax import lax
from jax.sharding import PartitionSpec as P

EXP_ROW = 2
SPAN = 4


epsilon = 1e-05


def shifted(shard, axis, by):
    devices = lax.axis_size(axis)
    pairs = [(i, i + by) for i in range(devices) if 0 <= i + by < devices]
    return lax.ppermute(shard, axis, pairs)


def root_norm(values, gain):
    mean_square = jnp.mean(values * values, axis=-1, keepdims=True)
    return values * lax.rsqrt(mean_square + epsilon) * gain


def body(
    tokens,
    attn_gain,
    w_query,
    w_key,
    w_value,
    w_out,
    moe_gain,
    expert_ids,
    route_weight,
    w_gate,
    w_up,
    w_down,
):
    tok_rows, model_width = tokens.shape
    head_size = w_query.shape[1]
    seq_count = lax.axis_size("seq")
    ep_count = lax.axis_size("ep")
    seq_place = lax.axis_index("seq")
    ep_place = lax.axis_index("ep")
    row_share = tok_rows // ep_count
    tok_float = tokens.astype(jnp.float32)
    normed = root_norm(tok_float, attn_gain).astype(jnp.bfloat16)
    query_vectors = jnp.dot(normed, w_query, preferred_element_type=jnp.float32).astype(
        jnp.bfloat16
    )
    keys = jnp.dot(normed, w_key, preferred_element_type=jnp.float32).astype(jnp.bfloat16)
    values = jnp.dot(normed, w_value, preferred_element_type=jnp.float32).astype(jnp.bfloat16)
    stacked = jnp.stack([keys, values])
    key_parts = []
    value_parts = []
    for distance in range(SPAN, 0, -1):
        earlier = shifted(stacked, "seq", distance)
        key_parts.append(earlier[0])
        value_parts.append(earlier[1])
    window_key_rows = jnp.concatenate(key_parts + [keys], axis=0)
    window_value_rows = jnp.concatenate(value_parts + [values], axis=0)
    attention_logits = lax.dot_general(
        query_vectors, window_key_rows, (((1,), (1,)), ((), ())), preferred_element_type=jnp.float32
    ) / math.sqrt(head_size)
    query_pos = jnp.arange(tok_rows, dtype=jnp.int32)[:, None]
    key_rel = jnp.arange((SPAN + 1) * tok_rows, dtype=jnp.int32)[None, :] - SPAN * tok_rows
    window_len = SPAN * tok_rows
    allowed = (
        (key_rel <= query_pos)
        & (key_rel > query_pos - window_len)
        & (seq_place * tok_rows + key_rel >= 0)
    )
    attention_logits = jnp.where(allowed, attention_logits, -1e30)
    peak = jnp.max(attention_logits, axis=-1, keepdims=True)
    expo = jnp.exp(attention_logits - peak)
    attention_probabilities = (expo / jnp.sum(expo, axis=-1, keepdims=True)).astype(jnp.bfloat16)
    attention_output = jnp.dot(
        attention_probabilities, window_value_rows, preferred_element_type=jnp.float32
    ).astype(jnp.bfloat16)
    head_terms = jnp.dot(attention_output, w_out, preferred_element_type=jnp.float32)
    attn_total = lax.psum(head_terms, "ep")
    residual = tok_float + attn_total
    moe_in = root_norm(residual, moe_gain).astype(jnp.bfloat16)
    resid_rows = lax.dynamic_slice_in_dim(residual, ep_place * row_share, row_share, 0)
    top_count = expert_ids.shape[1]
    experts_all = seq_count * EXP_ROW
    slices = ep_count // EXP_ROW
    expert_half = ep_place // slices
    capacity = tok_rows * top_count // experts_all + tok_rows // 32
    expert_iota = jnp.arange(experts_all, dtype=jnp.int32)
    chosen = (expert_ids[:, :, None] == expert_iota).astype(jnp.float32)
    counts = jnp.sum(chosen, axis=1)
    earlier_mask = (jnp.arange(tok_rows)[:, None] > jnp.arange(tok_rows)[None, :]).astype(
        jnp.float32
    )
    before = jnp.dot(
        earlier_mask, counts, precision=lax.Precision.HIGHEST, preferred_element_type=jnp.float32
    )
    slot_index = jnp.sum(chosen * before[:, None, :], axis=-1)
    own_pairs = expert_ids % EXP_ROW == expert_half
    flat_slot = (expert_ids // EXP_ROW).astype(jnp.float32) * capacity + slot_index
    slot_iota = jnp.arange(seq_count * capacity, dtype=jnp.float32)
    slot_hits = (flat_slot[:, :, None] == slot_iota) & own_pairs[:, :, None]
    dispatch = jnp.any(slot_hits, axis=1).astype(jnp.bfloat16)
    panels = lax.dot_general(
        dispatch, moe_in, (((0,), (0,)), ((), ())), preferred_element_type=jnp.float32
    )
    panels = panels.astype(jnp.bfloat16).reshape(seq_count, capacity, model_width)
    rate = route_weight.astype(jnp.bfloat16).astype(jnp.float32)
    combine = jnp.sum(jnp.where(slot_hits, rate[:, :, None], 0.0), axis=1).astype(jnp.bfloat16)
    arrived = lax.all_to_all(panels, "seq", split_axis=0, concat_axis=0, tiled=True)
    flat_rows = arrived.reshape(-1, model_width)
    gate = lax.dot_general(
        flat_rows, w_gate, (((1,), (1,)), ((), ())), preferred_element_type=jnp.float32
    )
    upward = lax.dot_general(
        flat_rows, w_up, (((1,), (1,)), ((), ())), preferred_element_type=jnp.float32
    )
    hidden = (jax.nn.silu(gate) * upward).astype(jnp.bfloat16)
    result = jnp.dot(hidden, w_down, preferred_element_type=jnp.float32).astype(jnp.bfloat16)
    expert_out = result.reshape(arrived.shape[0], arrived.shape[1], model_width)
    returned = lax.all_to_all(expert_out, "seq", split_axis=0, concat_axis=0, tiled=True)
    moe_terms = jnp.dot(
        combine, returned.reshape(-1, model_width), preferred_element_type=jnp.float32
    )
    moe_rows = lax.psum_scatter(moe_terms, "ep", scatter_dimension=0, tiled=True)
    return (resid_rows + moe_rows).astype(jnp.bfloat16)


def solution(mesh):
    in_specs = (
        P("seq", None),
        P(),
        P(None, "ep"),
        P(None, "ep"),
        P(None, "ep"),
        P("ep", None),
        P(),
        P("seq", None),
        P("seq", None),
        P(("seq", "ep"), None),
        P(("seq", "ep"), None),
        P(("seq", "ep"), None),
    )
    out_specs = P(("seq", "ep"), None)
    return jax.shard_map(body, mesh=mesh, in_specs=in_specs, out_specs=out_specs, check_vma=False)
```

profile of v0, /device:TPU:31, one launch (start us, length us, event | category | flops | bytes accessed | tf_op | source)
XLA Modules:
  0.0 207.9 jit_solution(13454979332110237027)
XLA Ops:
  6.6 1.3 fusion.5
  8.0 1.6 convolution_convert_fusion.4
  10.0 1.4 collective-permute-start
  11.5 1.3 collective-permute-start.1
  12.8 1.3 collective-permute-start.2
  14.1 1.3 collective-permute-start.3
  15.6 3.8 %collective-permute-done = bf16[2,128,128]{2,1,0:T(8,128)(2,1)S(1)} collective-permute-done((bf16[2,128,128]{2,1,0:T(8,128)(2,1)S(1)}, bf16[2,128,128]{2,1,0:T(8,128)(2,1)S(1)}, u32[]{:S(2)}, u32[]{:S(2)}) %collective-permute-start) | collective-permute-done | bytes 65568 | tf_op jit(solution)/shard_map/ppermute | solution.py:18
  21.0 1.6 fusion.4
  22.9 39.7 %all-reduce.2.cloned.1.call-done = f32[128,2048]{1,0:T(8,128)} async-done(((f32[128,2048]{1,0:T(8,128)}), f32[128,2048]{1,0:T(8,128)}) %all-reduce.2.cloned.1.call-update) | async-done | bytes 1048592 | tf_op jit(solution)/shard_map/psum | solution.py:82
  62.7 1.4 multiply_reduce_fusion
  64.1 1.0 copy-done.1
  65.1 1.9 convolution_convert_fusion.1
  67.0 1.6 reshape.52
  68.6 45.8 %all_to_all.10 = bf16[8,52,2048]{2,1,0:T(8,128)(2,1)} all-to-all(bf16[8,52,2048]{2,1,0:T(8,128)(2,1)S(1)} %reshape.52), channel_id=1, replica_groups=mesh['seq'=8,'ep'=4] {'seq'}, dimensions={0} | all-to-all | bytes 3407872 | tf_op jit(solution)/shard_map/all_to_all | solution.py:112
  114.3 1.7 reshape.53
  116.1 1.4 fusion.48
  117.5 3.9 %convolution_convert_fusion = bf16[416,2048]{1,0:T(8,128)(2,1)} fusion(bf16[176,2048]{1,0:T(8,128)(2,1)S(1)} %copy-done, bf16[416,2048]{1,0:T(8,128)(2,1)S(1)} %reshape.53, bf16[176,2048]{1,0:T(8,128)(2,1)} %param.22, f32[416,176]{0,1:T(8,128)} %fusion.48), kind=kOutput, calls=%fused_computation | convolution fusion | flops 601076736 | bytes 5142528 | tf_op jit(solution)/shard_map/dot_general | solution.py:121
  121.3 2.6 %reshape.54 = bf16[8,52,2048]{2,1,0:T(8,128)(2,1)} reshape(bf16[416,2048]{1,0:T(8,128)(2,1)} %convolution_convert_fusion) | data formatting | bytes 3407872 | tf_op jit(solution)/shard_map/reshape | solution.py:122
  123.9 5.6 %all-to-all-start.1 = ((bf16[8,52,2048]{2,1,0:T(8,128)(2,1)}), bf16[8,52,2048]{2,1,0:T(8,128)(2,1)S(1)}, u32[]{:S(2)}, u32[]{:S(2)}) async-start(bf16[8,52,2048]{2,1,0:T(8,128)(2,1)} %reshape.54), calls=%async_computation.1 | async-start | bytes 3670016 | tf_op jit(solution)/shard_map/all_to_all | solution.py:123
  129.8 40.7 %all-to-all-done.1 = bf16[8,52,2048]{2,1,0:T(8,128)(2,1)S(1)} async-done(((bf16[8,52,2048]{2,1,0:T(8,128)(2,1)}), bf16[8,52,2048]{2,1,0:T(8,128)(2,1)S(1)}, u32[]{:S(2)}, u32[]{:S(2)}) %all-to-all-start.1) | async-done | bytes 1703968 | tf_op jit(solution)/shard_map/all_to_all | solution.py:123
  170.5 1.4 reshape.55
  171.8 2.9 %fusion.49 = f32[128,2048]{1,0:T(8,128)} fusion(bf16[128,416]{0,1:T(8,128)(2,1)S(1)} %select_reduce_fusion, bf16[416,2048]{1,0:T(8,128)(2,1)} %reshape.55), kind=kOutput, calls=%fused_computation.87 | convolution fusion | flops 218103808 | bytes 2859008 | tf_op jit(solution)/shard_map/dot_general | solution.py:124
  174.8 24.6 %reduce-scatter.2.cloned.1.call-done = f32[32,2048]{1,0:T(8,128)} async-done(((f32[128,2048]{1,0:T(8,128)}), f32[32,2048]{1,0:T(8,128)}) %reduce-scatter.2.cloned.1.call-update) | async-done | bytes 262160 | tf_op jit(solution)/shard_map/reduce_scatter | solution.py:127
  199.4 1.7 add_convert_fusion
  (50 shorter events, 2.9 us)
Async XLA Ops:
  6.5 110.9 %copy-start = (bf16[176,2048]{1,0:T(8,128)(2,1)S(1)}, bf16[176,2048]{1,0:T(8,128)(2,1)}, u32[]{:S(2)}) copy-start(bf16[176,2048]{1,0:T(8,128)(2,1)} %param.23) | copy-start | bytes 2162692
  6.5 3.1 %copy-start.2 = (bf16[128,2048]{1,0:T(8,128)(2,1)S(1)}, bf16[128,2048]{1,0:T(8,128)(2,1)}, u32[]{:S(2)}) copy-start(bf16[128,2048]{1,0:T(8,128)(2,1)} %param.12) | copy-start | bytes 1572868
  6.5 3.1 %copy-start.10 = (f32[2048]{0:T(1024)S(1)}, f32[2048]{0:T(1024)}, u32[]{:S(2)}) copy-start(f32[2048]{0:T(1024)} %param.13) | copy-start | bytes 24580
  6.5 3.1 %copy-start.8 = (bf16[2048,128]{1,0:T(8,128)(2,1)S(1)}, bf16[2048,128]{1,0:T(8,128)(2,1)}, u32[]{:S(2)}) copy-start(bf16[2048,128]{1,0:T(8,128)(2,1)} %param.16) | copy-start | bytes 1572868
  6.5 8.9 %copy-start.4 = (s32[128,6]{0,1:T(8,128)S(1)}, s32[128,6]{0,1:T(8,128)}, u32[]{:S(2)}) copy-start(s32[128,6]{0,1:T(8,128)} %param.19) | copy-start | bytes 9220
  6.5 56.1 %all-reduce.2.cloned.1.call-start = ((), (), s32[]{:S(2)}) async-start(), calls=%async_computation.3 | async-start | bytes 2097152 | tf_op jit(solution)/shard_map/psum | solution.py:82
  8.0 12.2 %copy-start.9 = (bf16[2048,128]{1,0:T(8,128)(2,1)S(1)}, bf16[2048,128]{1,0:T(8,128)(2,1)}, u32[]{:S(2)}) copy-start(bf16[2048,128]{1,0:T(8,128)(2,1)} %param.14) | copy-start | bytes 1572868
  10.0 11.0 %copy-start.3 = (bf16[128,2048]{1,0:T(8,128)(2,1)S(1)}, bf16[128,2048]{1,0:T(8,128)(2,1)}, u32[]{:S(2)}) copy-start(bf16[128,2048]{1,0:T(8,128)(2,1)} %param.17) | copy-start | bytes 1572868
  10.0 9.3 %collective-permute-start = (bf16[2,128,128]{2,1,0:T(8,128)(2,1)S(1)}, bf16[2,128,128]{2,1,0:T(8,128)(2,1)S(1)}, u32[]{:S(2)}, u32[]{:S(2)}) collective-permute-start(bf16[2,128,128]{2,1,0:T(8,128)(2,1)S(1)} %pad_maximum_fusion), channel_id=1, source_target_pairs={{0,16},{4,20},{8,24},{12,28},{1,17},{5,21},{9,25},{13,29},{2,18},{... | collective-permute-start | bytes 196616 | tf_op jit(solution)/shard_map/ppermute | solution.py:18
  11.5 7.9 %collective-permute-start.1 = (bf16[2,128,128]{2,1,0:T(8,128)(2,1)S(1)}, bf16[2,128,128]{2,1,0:T(8,128)(2,1)S(1)}, u32[]{:S(2)}, u32[]{:S(2)}) collective-permute-start(bf16[2,128,128]{2,1,0:T(8,128)(2,1)S(1)} %pad_maximum_fusion), channel_id=1, source_target_pairs={{0,12},{4,16},{8,20},{12,24},{16,28},{1,13},{5,17},{9,21},{13,25},... | collective-permute-start | bytes 196616 | tf_op jit(solution)/shard_map/ppermute | solution.py:18
  12.8 6.6 %collective-permute-start.2 = (bf16[2,128,128]{2,1,0:T(8,128)(2,1)S(1)}, bf16[2,128,128]{2,1,0:T(8,128)(2,1)S(1)}, u32[]{:S(2)}, u32[]{:S(2)}) collective-permute-start(bf16[2,128,128]{2,1,0:T(8,128)(2,1)S(1)} %pad_maximum_fusion), channel_id=1, source_target_pairs={{0,8},{4,12},{8,16},{12,20},{16,24},{20,28},{1,9},{5,13},{9,17},{1... | collective-permute-start | bytes 196616 | tf_op jit(solution)/shard_map/ppermute | solution.py:18
  14.1 6.1 %collective-permute-start.3 = (bf16[2,128,128]{2,1,0:T(8,128)(2,1)S(1)}, bf16[2,128,128]{2,1,0:T(8,128)(2,1)S(1)}, u32[]{:S(2)}, u32[]{:S(2)}) collective-permute-start(bf16[2,128,128]{2,1,0:T(8,128)(2,1)S(1)} %pad_maximum_fusion), channel_id=1, source_target_pairs={{0,4},{4,8},{8,12},{12,16},{16,20},{20,24},{24,28},{1,5},{5,9},{9,... | collective-permute-start | bytes 196616 | tf_op jit(solution)/shard_map/ppermute | solution.py:18
  22.6 42.5 %copy-start.5 = (f32[2048]{0:T(1024)S(1)}, f32[2048]{0:T(1024)}, u32[]{:S(2)}) copy-start(f32[2048]{0:T(1024)} %param.18) | copy-start | bytes 24580
  64.1 1.0 copy-start.1
  114.3 1.7 copy-start.7
  123.9 5.6 %copy-start.6 = (f32[128,6]{0,1:T(8,128)S(1)}, f32[128,6]{0,1:T(8,128)}, u32[]{:S(2)}) copy-start(f32[128,6]{0,1:T(8,128)} %param.20) | copy-start | bytes 9220
  123.9 46.6 %all-to-all-start.1 = ((bf16[8,52,2048]{2,1,0:T(8,128)(2,1)}), bf16[8,52,2048]{2,1,0:T(8,128)(2,1)S(1)}, u32[]{:S(2)}, u32[]{:S(2)}) async-start(bf16[8,52,2048]{2,1,0:T(8,128)(2,1)} %reshape.54), calls=%async_computation.1 | async-start | bytes 3670016 | tf_op jit(solution)/shard_map/all_to_all | solution.py:123
  129.5 69.9 %reduce-scatter.2.cloned.1.call-start = ((), (), s32[]{:S(2)}) async-start(), calls=%async_computation.4 | async-start | bytes 1310720 | tf_op jit(solution)/shard_map/reduce_scatter | solution.py:127
Sparse Core Ops, SparseCore 0:
  22.8 39.8 all-reduce.1
  174.9 24.4 reduce-scatter.1
where the time goes:
time: 211 us; the launch traced here: 208 us
  waiting for transfers between devices  110 us (52%)
  blocking collectives  45.8 us (22%)
  matrix products  14.4 us (7%)
  between operations  13.7 us (6%)
  starting transfers between devices  10.9 us (5%)
  local copies, waits for them, and re-layouts  8.3 us (4%)
  other arithmetic  5.34 us (3%)
    all_to_all x1, blocking collectives, body(): lax.all_to_all(panels, 'seq', split_axis=0, concat_axis=0, tiled=True)  45.8 us
    all_to_all x1, waiting for transfers between devices, body(): lax.all_to_all(expert_out, 'seq', split_axis=0, concat_axis=0, tiled=True)  40.7 us
    psum x1, waiting for transfers between devices, body(): attn_total = lax.psum(head_terms, 'ep')  39.7 us
    reduce_scatter x1, waiting for transfers between devices, body(): lax.psum_scatter(moe_terms, 'ep', scatter_dimension=0, tiled=True)  24.6 us
    all_to_all x1, starting transfers between devices, body(): lax.all_to_all(expert_out, 'seq', split_axis=0, concat_axis=0, tiled=True)  5.57 us
    ppermute x4, starting transfers between devices, shifted(): return lax.ppermute(shard, axis, pairs)  5.3 us
    ppermute x4, waiting for transfers between devices, shifted(): return lax.ppermute(shard, axis, pairs)  4.55 us
  transfers between devices with their start and end apart: 7, of which 5 were waited for; matrix products, arithmetic and copies ran while one was open for 0% of the time, Pallas kernels for 0%

commit v1 on v0

v1 whole, which is shorter than its diff:
```python
import functools
import math

import jax
import jax.numpy as jnp
from jax import lax
from jax.experimental import pallas as pl
from jax.experimental.pallas import tpu as pltpu
from jax.sharding import PartitionSpec as P

EXP_ROW = 2
SPAN = 4
EPS = 1e-05
F32 = jnp.float32
BF16 = jnp.bfloat16
MESH = pl.DeviceIdType.MESH


def dot(a, b, dims=((1,), (0,))):
    return lax.dot_general(a, b, (dims, ((), ())), preferred_element_type=F32)


def kernel(
    S,
    E,
    cap,
    slots,
    tokens,
    attn_gain,
    w_query,
    w_key,
    w_value,
    w_out,
    moe_gain,
    ids_ref,
    route_ref,
    w_gate,
    w_up,
    w_down,
    out_ref,
    kv,
    wout,
    att,
    squares,
    squares_in,
    panels,
    arrived,
    passed,
    gate_w,
    up_w,
    down_w,
    halves,
    halves_in,
    summed,
    returned,
    part_far,
    part_near,
    far_in,
    near_in,
    wout_send,
    wout_recv,
    kv_send,
    kv_recv,
    att_send,
    att_recv,
    sq_sem,
    disp_send,
    disp_recv,
    pass_send,
    pass_recv,
    half_send,
    half_recv,
    ret_send,
    ret_recv,
    fin_send,
    fin_recv,
    load_sem,
):
    rows, width = tokens.shape
    head = w_query.shape[1]
    half = width // 2
    share = rows // E
    s = lax.axis_index("seq")
    e = lax.axis_index("ep")
    c = lax.rem(e, 2)
    mate = e + 1 - 2 * c
    own_cols = pl.ds(pl.multiple_of(c * half, 128), half)
    mate_cols = pl.ds(pl.multiple_of((1 - c) * half, 128), half)
    seq_peer = [lax.rem(s + r, S) for r in range(S)]
    ep_peer = [lax.rem(e + r, E) for r in range(E)]

    def remote(src, dst, send, recv, seq=None, ep=None):
        return pltpu.make_async_remote_copy(
            src_ref=src,
            dst_ref=dst,
            send_sem=send,
            recv_sem=recv,
            device_id=(s if seq is None else seq, e if ep is None else ep),
            device_id_type=MESH,
        )

    barrier = pltpu.get_barrier_semaphore()
    for r in range(1, S):
        pl.semaphore_signal(barrier, inc=1, device_id=(seq_peer[r], e), device_id_type=MESH)
    for r in range(1, E):
        pl.semaphore_signal(barrier, inc=1, device_id=(s, ep_peer[r]), device_id_type=MESH)

    loads = [
        pltpu.make_async_copy(w_gate, gate_w, load_sem.at[0]),
        pltpu.make_async_copy(w_up, up_w, load_sem.at[1]),
        pltpu.make_async_copy(w_down, down_w, load_sem.at[2]),
        pltpu.make_async_copy(
            w_out.at[:, own_cols],
            wout.at[pl.ds(pl.multiple_of(e * head, 128), head), :],
            load_sem.at[3],
        ),
    ]
    for copy in loads:
        copy.start()

    normed = tokens[...].astype(F32)
    mean_square = jnp.mean(normed * normed, axis=-1, keepdims=True)
    normed = (normed * lax.rsqrt(mean_square + EPS) * attn_gain[...]).astype(BF16)
    own_rows = pl.ds(SPAN * rows, rows)
    kv[own_rows, :head] = dot(normed, w_key[...]).astype(BF16)
    kv[own_rows, head:] = dot(normed, w_value[...]).astype(BF16)

    pl.semaphore_wait(barrier, S - 1 + E - 1)

    kv_copies = {}
    for d in range(1, SPAN + 1):
        kv_copies[d] = remote(
            kv.at[own_rows, :],
            kv.at[pl.ds((SPAN - d) * rows, rows), :],
            kv_send.at[d],
            kv_recv.at[d],
            seq=lax.rem(s + d, S),
        )

        @pl.when(s + d < S)
        def _(d=d):
            kv_copies[d].start()

    wout_copies = {}
    for r in range(1, E):
        peer = ep_peer[r]
        cols = pl.ds(pl.multiple_of(lax.rem(peer, 2) * half, 128), half)
        wout_copies[r] = remote(
            w_out.at[:, cols],
            wout.at[pl.ds(pl.multiple_of(e * head, 128), head), :],
            wout_send.at[r],
            wout_recv.at[r],
            ep=peer,
        )
        wout_copies[r].start()

    query = dot(normed, w_query[...]).astype(BF16)

    expert_half = e // (E // EXP_ROW)
    lane = lax.broadcasted_iota(jnp.int32, (rows, 128), 1)
    ids = ids_ref[...]
    rate = route_ref[...].astype(BF16).astype(F32)
    chosen = jnp.zeros((rows, 128), F32)
    rates = jnp.zeros((rows, 128), F32)
    for k in range(ids.shape[1]):
        hit = (ids[:, k : k + 1] == lane * EXP_ROW + expert_half) & (lane < S)
        chosen = jnp.where(hit, 1.0, chosen)
        rates = jnp.where(hit, rate[:, k : k + 1], rates)
    earlier = (
        lax.broadcasted_iota(jnp.int32, (rows, rows), 0)
        > lax.broadcasted_iota(jnp.int32, (rows, rows), 1)
    ).astype(F32)
    before = dot(earlier.astype(BF16), chosen.astype(BF16))
    place = jnp.where(chosen > 0.5, before, 255.0).astype(BF16)
    spread_row = lax.broadcasted_iota(jnp.int32, (128, S * slots), 0) * slots
    spread_lane = lax.broadcasted_iota(jnp.int32, (128, S * slots), 1)
    spread = jnp.where(
        (spread_lane >= spread_row) & (spread_lane < spread_row + slots), 1.0, 0.0
    ).astype(BF16)
    slot_of = (lax.broadcasted_iota(jnp.int32, (rows, S * slots), 1) % slots).astype(F32)
    filled = dot(place, spread) == slot_of
    dispatch = jnp.where(filled, 1.0, 0.0).astype(BF16)
    combine = jnp.where(filled, dot(rates.astype(BF16), spread), 0.0).astype(BF16)

    for d in range(1, SPAN + 1):

        @pl.when(s < d)
        def _(d=d):
            kv[pl.ds((SPAN - d) * rows, rows), :] = jnp.zeros((rows, 2 * head), BF16)

    for d in range(1, SPAN + 1):

        @pl.when(s >= d)
        def _(d=d):
            kv_copies[d].wait_recv()

    window = SPAN * rows
    logits = dot(query, kv[:, :head], ((1,), (1,))) / math.sqrt(head)
    query_pos = lax.broadcasted_iota(jnp.int32, logits.shape, 0)
    key_rel = lax.broadcasted_iota(jnp.int32, logits.shape, 1) - window
    allowed = (
        (key_rel <= query_pos) & (key_rel > query_pos - window) & (s * rows + key_rel >= 0)
    )
    logits = jnp.where(allowed, logits, -1e30)
    expo = jnp.exp(logits - jnp.max(logits, axis=-1, keepdims=True))
    probs = (expo / jnp.sum(expo, axis=-1, keepdims=True)).astype(BF16)
    own_head = pl.ds(pl.multiple_of(e * head, 128), head)
    att[:, own_head] = dot(probs, kv[:, head:]).astype(BF16)

    att_copies = {}
    for r in range(1, E):
        att_copies[r] = remote(
            att.at[:, own_head], att.at[:, own_head], att_send.at[r], att_recv.at[r], ep=ep_peer[r]
        )
        att_copies[r].start()
    loads[3].wait()
    for r in range(1, E):
        wout_copies[r].wait_recv()
    for r in range(1, E):
        att_copies[r].wait_recv()

    residual = tokens[:, own_cols].astype(F32) + dot(att[...], wout[...])
    partial = jnp.zeros((rows, 128), F32)
    for i in range(half // 128):
        piece = residual[:, i * 128 : (i + 1) * 128]
        partial = partial + piece * piece
    squares[...] = partial
    sq_copy = remote(squares, squares_in, sq_sem.at[0], sq_sem.at[1], ep=mate)
    sq_copy.start()
    sq_copy.wait_recv()
    mean_square = jnp.sum(partial + squares_in[...], axis=-1, keepdims=True) / width
    moe_in = (residual * lax.rsqrt(mean_square + EPS) * moe_gain[:, own_cols]).astype(BF16)
    panels[...] = (
        dot(dispatch, moe_in, ((0,), (0,))).reshape(S, slots, half).astype(BF16)
    )

    disp = {}
    for r in range(1, S):
        disp[r] = remote(
            panels.at[seq_peer[r]], arrived.at[s], disp_send.at[r], disp_recv.at[r], seq=seq_peer[r]
        )
        disp[r].start()
    arrived[s] = panels[s]

    passes = {}
    for r in range(S):
        source = lax.rem(s + S - r, S)
        if r:
            disp[r].wait_recv()
        passes[r] = remote(
            arrived.at[source], passed.at[source], pass_send.at[r], pass_recv.at[r], ep=mate
        )
        passes[r].start()
    for copy in loads[:3]:
        copy.wait()
    mine = arrived[...].astype(F32).reshape(S * slots, half).astype(BF16)
    gate = dot(mine, gate_w[:, own_cols], ((1,), (1,)))
    upward = dot(mine, up_w[:, own_cols], ((1,), (1,)))
    for r in range(S):
        passes[r].wait_recv()
    others = passed[...].astype(F32).reshape(S * slots, half).astype(BF16)
    gate = gate + dot(others, gate_w[:, mate_cols], ((1,), (1,)))
    upward = upward + dot(others, up_w[:, mate_cols], ((1,), (1,)))
    hidden = (gate / (1.0 + jnp.exp(-gate)) * upward).astype(BF16)

    halves[...] = dot(hidden, down_w[:, mate_cols]).reshape(S, slots, half).astype(BF16)
    half_copies = {}
    for r in range(S):
        half_copies[r] = remote(
            halves.at[seq_peer[r]],
            halves_in.at[seq_peer[r]],
            half_send.at[r],
            half_recv.at[r],
            ep=mate,
        )
        half_copies[r].start()
    result = dot(hidden, down_w[:, own_cols]).reshape(S, slots, half)
    for r in range(S):
        half_copies[r].wait_recv()
    summed[...] = (result + halves_in[...].astype(F32)).astype(BF16)
    ret = {}
    for r in range(1, S):
        ret[r] = remote(
            summed.at[seq_peer[r]], returned.at[s], ret_send.at[r], ret_recv.at[r], seq=seq_peer[r]
        )
        ret[r].start()
    returned[s] = summed[s]
    for r in range(1, S):
        ret[r].wait_recv()

    moe = dot(combine, returned[...].astype(F32).reshape(S * slots, half).astype(BF16))
    part_far[...] = moe.reshape(E, share, half).astype(BF16)
    part_near[...] = (moe + residual).reshape(E, share, half)
    fin_near = remote(
        part_near.at[mate], near_in, fin_send.at[0], fin_recv.at[0], ep=mate
    )
    fin_near.start()
    pair = e // 2
    fin_far = {}
    for r in range(1, E // 2):
        for other in range(2):
            peer = 2 * lax.rem(pair + r, E // 2) + other
            at = 2 * r + other
            fin_far[at] = remote(
                part_far.at[peer],
                far_in.at[r - 1, c],
                fin_send.at[at],
                fin_recv.at[2 * r + c],
                ep=peer,
            )
            fin_far[at].start()
    own = part_near[e]
    fin_near.wait_recv()
    near = near_in[...]
    sides = [jnp.where(c == 0, own, near), jnp.where(c == 0, near, own)]
    for r in range(1, E // 2):
        for other in range(2):
            arrival = remote(
                part_far.at[e],
                far_in.at[r - 1, other],
                fin_send.at[2 * r + other],
                fin_recv.at[2 * r + other],
                ep=mate,
            )
            arrival.wait_recv()
            sides[other] = sides[other] + far_in[r - 1, other].astype(F32)
    out_ref[:, :half] = sides[0].astype(BF16)
    out_ref[:, half:] = sides[1].astype(BF16)

    for d in range(1, SPAN + 1):

        @pl.when(s + d < S)
        def _(d=d):
            kv_copies[d].wait_send()

    sends = [sq_copy, fin_near]
    for group in (wout_copies, att_copies, disp, passes, half_copies, ret, fin_far):
        sends += list(group.values())
    for copy in sends:
        copy.wait_send()


def body(
    tokens,
    attn_gain,
    w_query,
    w_key,
    w_value,
    w_out,
    moe_gain,
    expert_ids,
    route_weight,
    w_gate,
    w_up,
    w_down,
):
    rows, width = tokens.shape
    head = w_query.shape[1]
    S = lax.axis_size("seq")
    E = lax.axis_size("ep")
    half = width // 2
    share = rows // E
    ff = w_gate.shape[0]
    cap = rows * expert_ids.shape[1] // (S * EXP_ROW) + rows // 32
    slots = -(-cap // 8) * 8
    vmem = pl.BlockSpec(memory_space=pltpu.VMEM)
    hbm = pl.BlockSpec(memory_space=pl.ANY)
    panel = pltpu.VMEM((S, slots, half), BF16)
    dma = pltpu.SemaphoreType.DMA
    return pl.pallas_call(
        functools.partial(kernel, S, E, cap, slots),
        out_shape=jax.ShapeDtypeStruct((share, width), BF16),
        in_specs=[vmem, vmem, vmem, vmem, vmem, hbm, vmem, vmem, vmem, hbm, hbm, hbm],
        out_specs=vmem,
        scratch_shapes=[
            pltpu.VMEM(((SPAN + 1) * rows, 2 * head), BF16),
            pltpu.VMEM((E * head, half), BF16),
            pltpu.VMEM((rows, E * head), BF16),
            pltpu.VMEM((rows, 128), F32),
            pltpu.VMEM((rows, 128), F32),
            panel,
            panel,
            panel,
            pltpu.VMEM((ff, width), BF16),
            pltpu.VMEM((ff, width), BF16),
            pltpu.VMEM((ff, width), BF16),
            panel,
            panel,
            panel,
            panel,
            pltpu.VMEM((E, share, half), BF16),
            pltpu.VMEM((E, share, half), F32),
            pltpu.VMEM((E // 2 - 1, 2, share, half), BF16),
            pltpu.VMEM((share, half), F32),
            dma((E,)),
            dma((E,)),
            dma((SPAN + 1,)),
            dma((SPAN + 1,)),
            dma((E,)),
            dma((E,)),
            dma((2,)),
            dma((S,)),
            dma((S,)),
            dma((S,)),
            dma((S,)),
            dma((S,)),
            dma((S,)),
            dma((S,)),
            dma((S,)),
            dma((E,)),
            dma((E,)),
            dma((4,)),
        ],
        compiler_params=pltpu.CompilerParams(
            collective_id=0, has_side_effects=True, vmem_limit_bytes=56 * 1024 * 1024
        ),
    )(
        tokens,
        attn_gain.reshape(1, width),
        w_query,
        w_key,
        w_value,
        w_out,
        moe_gain.reshape(1, width),
        expert_ids,
        route_weight,
        w_gate,
        w_up,
        w_down,
    )


def solution(mesh):
    in_specs = (
        P("seq", None),
        P(),
        P(None, "ep"),
        P(None, "ep"),
        P(None, "ep"),
        P("ep", None),
        P(),
        P("seq", None),
        P("seq", None),
        P(("seq", "ep"), None),
        P(("seq", "ep"), None),
        P(("seq", "ep"), None),
    )
    out_specs = P(("seq", "ep"), None)
    return jax.shard_map(body, mesh=mesh, in_specs=in_specs, out_specs=out_specs, check_vma=False)
```

time: 211 us -> 77.9 us (0.37); the launches traced: 208 us -> 77.7 us
  waiting for transfers between devices: 110 us -> 0 us
  Pallas kernels: 0 us -> 74 us
  blocking collectives: 45.8 us -> 0 us
  matrix products: 14.4 us -> 0 us
  between operations: 13.7 us -> 0.01 us
  starting transfers between devices: 10.9 us -> 0 us
  other arithmetic: 5.34 us -> 0 us
  local copies, waits for them, and re-layouts: 8.3 us -> 3.75 us
    pallas_call x0 -> x1, Pallas kernels: none -> 74 us  [body(): pl.pallas_call(functools.partial(kernel, S, E, cap, slots), out_shape=jax...]
    all_to_all x1 -> x0, blocking collectives: 45.8 us -> none  [body(): lax.all_to_all(panels, 'seq', split_axis=0, concat_axis=0, tiled=True)]
    all_to_all x1 -> x0, waiting for transfers between devices: 40.7 us -> none  [body(): lax.all_to_all(expert_out, 'seq', split_axis=0, concat_axis=0, tiled=True)]
    psum x1 -> x0, waiting for transfers between devices: 39.7 us -> none  [body(): attn_total = lax.psum(head_terms, 'ep')]
    reduce_scatter x1 -> x0, waiting for transfers between devices: 24.6 us -> none  [body(): lax.psum_scatter(moe_terms, 'ep', scatter_dimension=0, tiled=True)]
    dot_general x9 -> x0, matrix products: 14.4 us -> none  [the longest x1 3.86 us: body(): jnp.dot(hidden, w_down, preferred_element_type=jnp.float32)]
    reshape x4 -> x0, local copies, waits for them, and re-layouts: 7.23 us -> none  [the longest x1 2.59 us: body(): expert_out = result.reshape(arrived.shape[0], arrived.shape[1], model_width)]
    all_to_all x1 -> x0, starting transfers between devices: 5.57 us -> none  [body(): lax.all_to_all(expert_out, 'seq', split_axis=0, concat_axis=0, tiled=True)]
  transfers between devices with their start and end apart: 7 -> 0, of which waited for: 5 -> 0; matrix products, arithmetic and copies ran while one was open for 0% -> 0% of each run, Pallas kernels for 0% -> 0%
where the time goes in v1:
time: 77.9 us; the launch traced here: 77.7 us
  Pallas kernels  74 us (95%)
  local copies, waits for them, and re-layouts  3.75 us (5%)
    pallas_call x1, Pallas kernels, body(): pl.pallas_call(functools.partial(kernel, S, E, cap, slots), out_shape=jax...  74 us
    unnamed x5, local copies, waits for them, and re-layouts  3.75 us

profile of v1, /device:TPU:31, one launch (start us, length us, event | category | flops | bytes accessed | tf_op | source)
XLA Modules:
  0.0 77.7 jit_solution(2066738764133061452)
XLA Ops:
  0.0 0.0 copy-start
  0.0 1.4 %copy.13.ids_ref = s32[128,6]{1,0:T(8,128)} copy(s32[128,6]{0,1:T(8,128)} %param.19) | data formatting | bytes 6144 | tf_op args[7]
  1.4 0.0 copy-done
  1.4 0.7 copy.14.route_ref
  2.2 74.0 %shard_map.118 = bf16[32,2048]{1,0:T(8,128)(2,1)} custom-call(bf16[128,2048]{1,0:T(8,128)(2,1)} %tokens.1, f32[1,2048]{1,0:T(1,128)} %bitcast.2, bf16[2048,128]{1,0:T(8,128)(2,1)} %w_query.1, bf16[2048,128]{1,0:T(8,128)(2,1)} %w_key.1, bf16[2048,128]{1,0:T(8,128)(2,1)} %w_value.1, bf16[128,2048]{1,0:T(8,128)(2,1)} %w_out.1, f32[1,2048]{1,0:T(1,128)} %bitcast.3, ...), custom_call_target="tpu_custom_call" | custom-call | tf_op jit(solution)/shard_map/pallas_call | solution.py:370
  76.2 1.6 %copy.16 = bf16[32,2048]{1,0:T(8,128)(2,1)} copy(bf16[32,2048]{1,0:T(8,128)(2,1)} %shard_map.118) | data formatting | bytes 262144
Async XLA Ops:
  0.0 1.4 %copy-start = (f32[128,6]{0,1:T(8,128)S(1)}, f32[128,6]{0,1:T(8,128)}, u32[]{:S(2)}) copy-start(f32[128,6]{0,1:T(8,128)} %param.20) | copy-start | bytes 9220
